TPU v7x, 256 devices: a whole 4x4x8 slice. The times are simulated.
256 devices in a mesh: doc: 64 (over z, y, core), tp: 4 (over x).
Axes of the slice: x: 4, y: 4, z: 8, core: 2. Of those that a mesh axis runs over, the one named last changes fastest.
Arguments:
- storage: bfloat16 [32768, 3584], P('doc', 'tp'), may hold values from -40 to 40
- row_doc: int32 [32768], P('doc'), may hold values from -1 to 63, as said below
- row_pos: int32 [32768], P('doc'), may hold values from -1 to 511, as said below
- doc_len: int32 [64], replicated, may hold values from 64 to 512, as said below
- partner: int32 [64], replicated, may hold values from 0 to 63, as said below
- norm_gain: bfloat16 [3584], replicated, may hold values from 0.25 to 1.75
- qkv_weight: bfloat16 [3584, 4608], P('doc', 'tp'), may hold values from -0.09375 to 0.09375
- qkv_bias: bfloat16 [4608], P('tp'), may hold values from -24 to 24
Outputs:
- attention: bfloat16 [65536, 3584], P('doc', 'tp')
Inputs may be any that keep to these rules, and one draw needn't show every extreme that they name: `row_doc`: the rows 0 to doc_len[d] - 1 of each document d are stored exactly once over all devices, one to a slot; -1 marks an empty slot. One device stores at most 8 rows of any one document, and exactly 8 rows of a document of 512 tokens. `row_pos`: -1 for an empty slot. `doc_len`: some document has 512 tokens and some has 64. partner[partner[d]] = d and partner[d] != d.
All inputs are finite; a program needn't handle non-finite values.
Results may differ from a plain program's by a relative error of at most 0.008.
The roundings to bfloat16 on the way count: a program that leaves them out, or rounds other values in their place, can miss the bound.
Values may be sent and summed in bfloat16 or wider, within the bound.
A program may use at most 64 MiB of HBM per device.

v0:
```python
import jax
import jax.numpy as jnp
from jax import lax
from jax.sharding import PartitionSpec as P

HEADS = 28
KVH = 4
HD = 128
HALF = 512
ROPE_BASE = 1000000.0
EPSILON = 1e-06
BLOCK_ROWS = 512


def from_partner(value, axis, stride):
    mask = 2**stride
    pairs = [(source, source ^ mask) for source in range(lax.axis_size(axis))]
    return lax.ppermute(value, axis, pairs)


def pairing(partner):
    doc_ids = jnp.arange(partner.shape[0], dtype=jnp.int32)
    first_flag = (doc_ids < partner).astype(jnp.int32)
    before = jnp.cumsum(first_flag) - first_flag
    low_doc = jnp.minimum(doc_ids, partner)
    pick_mask = (low_doc[:, None] == doc_ids[None, :]).astype(jnp.int32)
    pair_index = jnp.sum(pick_mask * before[None, :], axis=1)
    scorer = 2 * pair_index + 1 - first_flag
    match_mask = (scorer[None, :] == doc_ids[:, None]).astype(jnp.int32)
    own_doc = jnp.sum(match_mask * doc_ids[None, :], axis=1)
    return (scorer, own_doc)


def rope_tables(length, head_dim):
    half_dim = head_dim // 2
    freq_ids = jnp.arange(half_dim, dtype=jnp.float32)
    inv_freq = jnp.exp(-(2.0 * freq_ids / head_dim) * jnp.log(jnp.float32(ROPE_BASE)))
    angles = jnp.arange(length, dtype=jnp.float32)[:, None] * inv_freq[None, :]
    cosine = jnp.concatenate([jnp.cos(angles), jnp.cos(angles)], axis=1)
    sine_table = jnp.concatenate([jnp.sin(angles), jnp.sin(angles)], axis=1)
    return (cosine, sine_table)


def rotate(heads, cosine, sine_table):
    widened = heads.astype(jnp.float32)
    half_dim = widened.shape[-1] // 2
    turned = jnp.concatenate([-widened[..., half_dim:], widened[..., :half_dim]], axis=-1)
    return (widened * cosine[:, None, :] + turned * sine_table[:, None, :]).astype(jnp.bfloat16)


def rms_norm(row_values, norm_gain):
    widened = row_values.astype(jnp.float32)
    inv_rms = lax.rsqrt(jnp.mean(widened * widened, axis=-1, keepdims=True) + EPSILON)
    return (widened * inv_rms * norm_gain.astype(jnp.float32)).astype(jnp.bfloat16)


def place_rows(values, dest_index, length):
    blank_rows = jnp.zeros((length,) + values.shape[1:], values.dtype)
    return blank_rows.at[dest_index].set(values, mode="drop")


def assemble(first_part, second_part, first_len):
    padded = jnp.concatenate([first_part, jnp.zeros_like(second_part)], axis=0)
    return lax.dynamic_update_slice(padded, second_part, (first_len, jnp.int32(0)))


def attention(projected, total_len, q_heads, kv_heads, head_dim):
    length = projected.shape[0]
    cosine, sine_table = rope_tables(length, head_dim)
    queries = rotate(
        projected[:, : q_heads * head_dim].reshape(length, q_heads, head_dim), cosine, sine_table
    )
    key_heads = rotate(
        projected[:, q_heads * head_dim : (q_heads + kv_heads) * head_dim].reshape(
            length, kv_heads, head_dim
        ),
        cosine,
        sine_table,
    )
    value_heads = projected[:, (q_heads + kv_heads) * head_dim :].reshape(
        length, kv_heads, head_dim
    )
    grouped = queries.reshape(length, kv_heads, q_heads // kv_heads, head_dim)
    block_length = min(BLOCK_ROWS, length)
    root_dim = jnp.sqrt(jnp.float32(head_dim))
    pieces = []
    for row_start in range(0, length, block_length):
        row_stop = row_start + block_length
        scores = (
            jnp.einsum(
                "qkgd,skd->kgqs",
                grouped[row_start:row_stop],
                key_heads[:row_stop],
                preferred_element_type=jnp.float32,
            )
            / root_dim
        )
        row_ids = jnp.arange(row_start, row_stop, dtype=jnp.int32)[:, None]
        col_ids = jnp.arange(row_stop, dtype=jnp.int32)[None, :]
        allowed = (col_ids <= row_ids) & (col_ids < total_len)
        scores = jnp.where(allowed, scores, -jnp.inf)
        largest = jnp.max(scores, axis=-1, keepdims=True)
        exponent = jnp.exp(scores - largest)
        probabilities = (exponent / jnp.sum(exponent, axis=-1, keepdims=True)).astype(jnp.bfloat16)
        mixture = jnp.einsum(
            "kgqs,skd->qkgd",
            probabilities,
            value_heads[:row_stop],
            preferred_element_type=jnp.float32,
        )
        live_rows = (jnp.arange(row_start, row_stop, dtype=jnp.int32) < total_len)[
            :, None, None, None
        ]
        mixture = jnp.where(live_rows, mixture, 0.0)
        pieces.append(mixture.astype(jnp.bfloat16).reshape(block_length, q_heads * head_dim))
    return jnp.concatenate(pieces, axis=0)


def shards(storage, row_doc, row_pos, doc_len, partner, norm_gain, qkv_weight, qkv_bias):
    doc_count = lax.axis_size("doc")
    me_index = lax.axis_index("doc")
    half_rows = HALF
    per_dest = half_rows // doc_count
    scorer, own_doc = pairing(partner)
    doc_ids = jnp.arange(doc_count, dtype=jnp.int32)
    first_doc = jnp.sum(jnp.where(doc_ids == me_index, own_doc, 0))
    second_doc = jnp.sum(jnp.where(doc_ids == first_doc, partner, 0))
    first_len = jnp.sum(jnp.where(doc_ids == first_doc, doc_len, 0))
    second_len = jnp.sum(jnp.where(doc_ids == second_doc, doc_len, 0))
    total_len = first_len + second_len
    stored = row_doc >= 0
    dest_scorer = jnp.sum(
        jnp.where(row_doc[:, None] == doc_ids[None, :], scorer[None, :], 0), axis=1
    )
    onehot = ((dest_scorer[:, None] == doc_ids[None, :]) & stored[:, None]).astype(jnp.int32)
    dest_rank = jnp.sum(jnp.cumsum(onehot, axis=0) * onehot, axis=1) - 1
    dest_index = jnp.where(stored, dest_scorer * per_dest + dest_rank, doc_count * per_dest)
    send_rows = place_rows(storage, dest_index, doc_count * per_dest).reshape(
        doc_count, per_dest, storage.shape[1]
    )
    send_pos = (
        jnp.full((doc_count * per_dest,), half_rows, jnp.int32)
        .at[dest_index]
        .set(row_pos, mode="drop")
    )
    send_pos = send_pos.reshape(doc_count, per_dest)
    got_rows, got_pos = (
        lax.all_to_all(send_rows, "doc", split_axis=0, concat_axis=0, tiled=True),
        lax.all_to_all(send_pos, "doc", split_axis=0, concat_axis=0, tiled=True),
    )
    own_rows = place_rows(
        got_rows.reshape(doc_count * per_dest, storage.shape[1]), got_pos.reshape(-1), half_rows
    )
    q_heads = HEADS // lax.axis_size("tp")
    kv_heads = KVH // lax.axis_size("tp")
    bias_wide = qkv_bias.astype(jnp.float32)
    other_rows = from_partner(own_rows, "doc", 0)
    both_full = lax.all_gather(
        jnp.concatenate([own_rows, other_rows], axis=0), "tp", axis=1, tiled=True
    )
    normed = rms_norm(both_full, norm_gain)
    full_weight = lax.all_gather(qkv_weight, "doc", axis=0, tiled=True)
    both_sum = jnp.dot(normed, full_weight, preferred_element_type=jnp.float32)
    both_proj = (both_sum + bias_wide).astype(jnp.bfloat16)
    projected = assemble(both_proj[:half_rows], both_proj[half_rows:], first_len)
    return attention(projected, total_len, q_heads, kv_heads, HD)


def solution(mesh):
    placed = (P("doc", "tp"), P("doc"), P("doc"), P(), P(), P(), P("doc", "tp"), P("tp"))
    return jax.shard_map(
        shards, mesh=mesh, in_specs=placed, out_specs=P("doc", "tp"), check_vma=False
    )
```

profile of v0, /device:TPU:1, one launch (start us, length us, event | category | flops | bytes accessed | tf_op | source)
XLA Modules:
  0.0 322.1 jit_solution(13756107359092494782)
XLA Ops:
  6.5 0.7 fusion.61
  7.2 0.7 broadcast_compare_fusion
  7.9 0.7 fusion.55
  8.6 0.1 copy.44
  8.7 0.1 reduce-window.19
  8.8 0.1 reduce.4
  8.9 0.7 iota_minimum_fusion
  9.5 0.2 select_reduce_fusion.2
  9.7 0.7 add_subtract_fusion
  10.4 0.8 select_reduce_fusion
  11.2 1.2 reduce-window.20
  12.4 0.2 slice_reduce_fusion
  12.7 0.1 fusion.44
  12.8 0.7 compare_select_fusion.1
  13.5 2.6 scatter_custom_fusion
  16.1 0.7 all_to_all.9
  16.8 13.2 %all-to-all-start = ((s32[64,1,8]{2,1,0:T(1,128)}), s32[64,1,8]{2,1,0:T(1,128)S(1)}, u32[]{:S(2)}, u32[]{:S(2)}) async-start(s32[64,1,8]{2,1,0:T(1,128)} %bitcast.4), calls=%async_computation | async-start | bytes 65536 | tf_op jit(solution)/shard_map/all_to_all | solution.py:149
  29.9 4.3 %scatter_custom_fusion.1 = bf16[512,896]{1,0:T(8,128)(2,1)} fusion(s32[512]{0:T(512)S(1)} %compare_select_fusion.1, bf16[512,896]{1,0:T(8,128)(2,1)} %param.8, bf16[]{:T(256)} %constant.24.clone.1), kind=kCustom, calls=%fused_computation.63 | custom fusion | bytes 918016 | tf_op jit(solution)/shard_map/scatter | solution.py:59
  34.2 5.1 %all-to-all-done = s32[64,1,8]{2,1,0:T(1,128)S(1)} async-done(((s32[64,1,8]{2,1,0:T(1,128)}), s32[64,1,8]{2,1,0:T(1,128)S(1)}, u32[]{:S(2)}, u32[]{:S(2)}) %all-to-all-start) | async-done | bytes 2080 | tf_op jit(solution)/shard_map/all_to_all | solution.py:149
  39.3 5.2 %all-to-all-start.1 = ((bf16[64,8,896]{2,1,0:T(8,128)(2,1)}), bf16[64,8,896]{2,1,0:T(8,128)(2,1)S(1)}, u32[]{:S(2)}, u32[]{:S(2)}) async-start(bf16[64,8,896]{2,1,0:T(8,128)(2,1)} %bitcast.6), calls=%async_computation.1 | async-start | bytes 1835008 | tf_op jit(solution)/shard_map/all_to_all | solution.py:148
  44.5 0.0 all-gather.3.cloned.1.call-start
  44.6 0.6 broadcast.173
  45.1 0.8 reduce.10
  45.9 0.1 reshape.211
  46.0 23.8 %all-to-all-done.1 = bf16[64,8,896]{2,1,0:T(8,128)(2,1)S(1)} async-done(((bf16[64,8,896]{2,1,0:T(8,128)(2,1)}), bf16[64,8,896]{2,1,0:T(8,128)(2,1)S(1)}, u32[]{:S(2)}, u32[]{:S(2)}) %all-to-all-start.1) | async-done | bytes 917536 | tf_op jit(solution)/shard_map/all_to_all | solution.py:148
  69.8 2.9 scatter_custom_fusion.2
  72.8 1.3 collective-permute-start
  74.1 2.1 collective-permute-done
  76.2 1.4 pad_maximum_fusion
  77.6 0.0 all-gather.3.cloned.1.call-update
  77.6 0.2 all-gather.5.cloned.1.call-start
  77.8 0.5 all-gather.5.cloned.1.call-update
  78.4 0.1 select_reduce_fusion.1
  78.5 0.6 fusion.52
  79.1 1.2 fusion.51
  80.4 1.8 fusion.53
  85.1 0.1 fusion.27
  85.2 0.4 fusion.20
  85.6 1.9 fusion.38
  87.6 0.0 copy-start.5
  87.6 63.3 %all-gather.3.cloned.1.call-done = bf16[1024,3584]{1,0:T(8,128)(2,1)} async-done(((bf16[1024,896]{1,0:T(8,128)(2,1)}), bf16[1024,3584]{1,0:T(8,128)(2,1)}) %all-gather.3.cloned.1.call-update) | async-done | bytes 7340048 | tf_op jit(solution)/shard_map/all_gather | solution.py:158
  150.9 4.6 %fusion = f32[1024]{0:T(1024)S(1)} fusion(bf16[1024,3584]{1,0:T(8,128)(2,1)} %all-gather.3.cloned.1.call-done), kind=kLoop, calls=%fused_computation.5 | loop fusion | flops 11009024 | bytes 7344128 | tf_op jit(solution)/shard_map/reduce_sum | solution.py:53
  155.5 82.3 %all-gather.5.cloned.1.call-done = bf16[3584,1152]{1,0:T(8,128)(2,1)} async-done(((bf16[56,1152]{1,0:T(8,128)(2,1)}), bf16[3584,1152]{1,0:T(8,128)(2,1)}) %all-gather.5.cloned.1.call-update) | async-done | bytes 8257552 | tf_op jit(solution)/shard_map/all_gather | solution.py:162
  237.8 15.6 %broadcast_select_fusion = (bf16[1024,1152]{1,0:T(8,128)(2,1)}, bf16[1024,1152]{1,0:T(8,128)(2,1)S(1)}) fusion(pred[1024]{0:T(1024)(128)(4,1)S(1)} %copy-done.5, f32[1152]{0:T(1024)S(1)} %convert_element_type.67, bf16[3584,1152]{1,0:T(8,128)(2,1)} %all-gather.5.cloned.1.call-done, bf16[1024,3584]{1,0:T(8,128)(2,1)} %all-gather.3.cloned.1.call-done, ...), kind=kOutput, calls=%fused_computation.31 | convolution fusion | flops 8473935872 | bytes 20340224 | tf_op jit(solution)/shard_map/dot_general | solution.py:163
  253.3 0.1 slice.64
  253.4 6.3 %dynamic_update_slice.3 = bf16[1024,1152]{1,0:T(8,128)(2,1)} dynamic-update-slice(bf16[1024,1152]{1,0:T(8,128)(2,1)} %get-tuple-element.18, bf16[512,1152]{1,0:T(8,128)(2,1)S(1)} %slice.64, s32[]{:T(128)S(6)} %select_n.63, s32[]{:T(128)} %constant.20.clone.1) | dynamic-update-slice | bytes 2359300 | tf_op jit(solution)/shard_map/dynamic_update_slice | solution.py:64
  259.8 1.0 convert_bitcast_fusion
  260.8 3.6 %slice_convert_fusion = f32[1024,896]{1,0:T(8,128)} fusion(bf16[1024,1152]{1,0:T(8,128)(2,1)} %dynamic_update_slice.3), kind=kLoop, calls=%fused_computation.34 | loop fusion | flops 917504 | bytes 5505024 | tf_op jit(solution)/shard_map/convert_element_type | solution.py:45
  264.3 0.2 fusion.36
  264.5 5.1 %copy.47 = f32[1024,896]{0,1:T(8,128)} copy(f32[1024,896]{1,0:T(8,128)} %slice_convert_fusion) | data formatting | bytes 7340032 | tf_op jit(solution)/shard_map/convert_element_type | solution.py:45
  269.6 5.0 %copy.48 = f32[1024,7,128]{2,0,1:T(8,128)} copy(f32[1024,7,128]{0,2,1:T(8,128)} %bitcast.104) | data formatting | bytes 7340032 | tf_op jit(solution)/shard_map/convert_element_type | solution.py:45
  274.6 4.4 %slice_negate_fusion = (f32[1024,7,64]{2,0,1:T(8,128)S(1)}, f32[1024,7,64]{2,0,1:T(8,128)S(1)}) fusion(f32[1024,7,128]{2,0,1:T(8,128)} %copy.48), kind=kLoop, calls=%fused_computation.24 | loop fusion | flops 458752 | bytes 7340032 | tf_op jit(solution)/shard_map/neg | solution.py:47
  279.0 1.6 fusion.35
  280.6 0.5 copy-done
  281.1 1.1 fusion.16
  282.3 1.3 fusion.12
  283.5 1.5 fusion.11
  285.1 4.0 %fusion.22 = bf16[1,128,7,512]{3,1,2,0:T(8,128)(2,1)} fusion(f32[7,512]{1,0:T(8,128)S(1)} %fusion.11, f32[7,512]{1,0:T(8,128)S(1)} %get-tuple-element.22, f32[512,512,7]{1,0,2:T(8,128)S(1)} %get-tuple-element.23, pred[512,512]{0,1:T(8,128)(4,1)S(1)} %fusion.27, pred[512]{0:T(512)(128)(4,1)S(1)} %get-tuple-element.24, bf16[1024,1152]{1,0:T(8,128)(2,1)} %dynamic_update_slice.3), kind=kOutput, calls=%fused_computation.40 | convolution fusion | flops 479854592 | bytes 8679936 | tf_op jit(solution)/shard_map/kgqs,skd->qkgd/dot_general | solution.py:105
  289.1 1.5 copy.55
  290.7 6.8 %fusion.4 = (f32[7,512]{1,0:T(8,128)S(1)}, f32[1024,512,7]{1,0,2:T(8,128)}) fusion(pred[512,1024]{0,1:T(8,128)(4,1)S(1)} %fusion.20, bf16[1024,7,128]{2,0,1:T(8,128)(2,1)S(1)} %fusion.16, bf16[1024,128]{1,0:T(8,128)(2,1)S(1)} %get-tuple-element.9), kind=kOutput, calls=%fused_computation.12 | convolution fusion | flops 950530560 | bytes 16398336 | tf_op jit(solution)/shard_map/qkgd,skd->kgqs/dot_general | solution.py:90
  297.4 8.2 %fusion.3 = f32[7,512]{1,0:T(8,128)S(1)} fusion(f32[1024,512,7]{1,0,2:T(8,128)} %get-tuple-element.21, f32[7,512]{1,0:T(8,128)S(1)} %get-tuple-element.20, pred[512,1024]{0,1:T(8,128)(4,1)S(1)} %fusion.20), kind=kLoop, calls=%fused_computation.11 | loop fusion | flops 14676480 | bytes 15233024 | tf_op jit(solution)/shard_map/reduce_sum | solution.py:104
  305.6 7.7 %fusion.21 = bf16[1,128,7,512]{3,1,2,0:T(8,128)(2,1)S(1)} fusion(f32[7,512]{1,0:T(8,128)S(1)} %fusion.3, f32[7,512]{1,0:T(8,128)S(1)} %get-tuple-element.20, f32[1024,512,7]{1,0,2:T(8,128)} %get-tuple-element.21, pred[512,1024]{0,1:T(8,128)(4,1)S(1)} %fusion.20, pred[512]{0:T(512)(128)(4,1)S(1)} %get-tuple-element.25, ...), kind=kOutput, calls=%fused_computation.38 | convolution fusion | flops 958791680 | bytes 16413184 | tf_op jit(solution)/shard_map/kgqs,skd->qkgd/dot_general | solution.py:105
  313.3 0.6 copy.56
  313.9 1.4 pad_maximum_fusion.1
  (21 shorter events, 0.1 us)
Async XLA Ops:
  16.8 22.5 %all-to-all-start = ((s32[64,1,8]{2,1,0:T(1,128)}), s32[64,1,8]{2,1,0:T(1,128)S(1)}, u32[]{:S(2)}, u32[]{:S(2)}) async-start(s32[64,1,8]{2,1,0:T(1,128)} %bitcast.4), calls=%async_computation | async-start | bytes 65536 | tf_op jit(solution)/shard_map/all_to_all | solution.py:149
  39.3 30.5 %all-to-all-start.1 = ((bf16[64,8,896]{2,1,0:T(8,128)(2,1)}), bf16[64,8,896]{2,1,0:T(8,128)(2,1)S(1)}, u32[]{:S(2)}, u32[]{:S(2)}) async-start(bf16[64,8,896]{2,1,0:T(8,128)(2,1)} %bitcast.6), calls=%async_computation.1 | async-start | bytes 1835008 | tf_op jit(solution)/shard_map/all_to_all | solution.py:148
  44.5 106.4 %all-gather.3.cloned.1.call-start = ((), (), s32[]{:S(2)}) async-start(), calls=%async_computation.2 | async-start | bytes 9175040 | tf_op jit(solution)/shard_map/all_gather | solution.py:158
  69.8 8.5 %copy-start.1 = (bf16[3584]{0:T(1024)(128)(2,1)S(1)}, bf16[3584]{0:T(1024)(128)(2,1)}, u32[]{:S(2)}) copy-start(bf16[3584]{0:T(1024)(128)(2,1)} %param.13) | copy-start | bytes 21508
  69.8 8.6 %copy-start.2 = (bf16[1152]{0:T(1024)(128)(2,1)S(1)}, bf16[1152]{0:T(1024)(128)(2,1)}, u32[]{:S(2)}) copy-start(bf16[1152]{0:T(1024)(128)(2,1)} %param.15) | copy-start | bytes 6916
  69.8 9.3 %copy-start.4 = (s32[64]{0:T(128)S(1)}, s32[64]{0:T(128)}, u32[]{:S(2)}) copy-start(s32[64]{0:T(128)} %param.12) | copy-start | bytes 772
  69.8 10.6 %copy-start.3 = (s32[64]{0:T(128)S(1)}, s32[64]{0:T(128)}, u32[]{:S(2)}) copy-start(s32[64]{0:T(128)} %param.11) | copy-start | bytes 772
  72.8 3.4 %collective-permute-start = (bf16[512,896]{1,0:T(8,128)(2,1)S(1)}, bf16[512,896]{1,0:T(8,128)(2,1)S(1)}, u32[]{:S(2)}, u32[]{:S(2)}) collective-permute-start(bf16[512,896]{1,0:T(8,128)(2,1)S(1)} %scatter_custom_fusion.2), channel_id=1, source_target_pairs={{0,4},{4,0},{8,12},{12,8},{16,20},{20,16},{24,28},{28,24},{32,36},... | collective-permute-start | bytes 2752520 | tf_op jit(solution)/shard_map/ppermute | solution.py:18
  77.6 160.2 %all-gather.5.cloned.1.call-start = ((), (), s32[]{:S(2)}) async-start(), calls=%async_computation.3 | async-start | bytes 8386560 | tf_op jit(solution)/shard_map/all_gather | solution.py:162
  87.6 150.2 %copy-start.5 = (pred[1024]{0:T(1024)(128)(4,1)S(1)}, pred[1024]{0:T(1024)(128)(4,1)}, u32[]{:S(2)}) copy-start(pred[1024]{0:T(1024)(128)(4,1)} %constant.16.clone.1) | copy-start | bytes 3076
  279.0 2.1 copy-start
Sparse Core Ops, SparseCore 0:
  77.7 73.1 all-gather.2
  153.6 84.1 all-gather.4
where the time goes:
time: 323 us; the launch traced here: 322 us
  waiting for transfers between devices  177 us (55%)
  other arithmetic  42.6 us (13%)
  matrix products  35.3 us (11%)
  local copies, waits for them, and re-layouts  30.7 us (10%)
  starting transfers between devices  19.9 us (6%)
  between operations  16.5 us (5%)
    all_gather x1, waiting for transfers between devices, shards(): full_weight = lax.all_gather(qkv_weight, 'doc', axis=0, tiled=True)  82.3 us
    all_gather x1, waiting for transfers between devices, shards(): lax.all_gather(jnp.concatenate([own_rows, other_rows], axis=0), 'tp', axi...  63.3 us
    all_to_all x1, waiting for transfers between devices, shards(): lax.all_to_all(send_rows, 'doc', split_axis=0, concat_axis=0, tiled=True)  23.8 us
    dot_general x1, matrix products, shards(): both_sum = jnp.dot(normed, full_weight, preferred_element_type=jnp.float32)  15.6 us
    all_to_all x1, starting transfers between devices, shards(): lax.all_to_all(send_pos, 'doc', split_axis=0, concat_axis=0, tiled=True)  13.2 us
    dot_general x2, matrix products, attention(): jnp.einsum('kgqs,skd->qkgd', probabilities, value_heads[:row_stop], prefe...  11.7 us
    convert_element_type x2, local copies, waits for them, and re-layouts, rotate(): widened = heads.astype(jnp.float32)  10.1 us
    reduce_sum x2, other arithmetic, attention(): jnp.sum(exponent, axis=-1, keepdims=True)  9.7 us
  transfers between devices with their start and end apart: 5, of which 5 were waited for; matrix products, arithmetic and copies ran while one was open for 5% of the time, Pallas kernels for 0%

commit v1 on v0

--- a/solution.py
+++ b/solution.py
@@ -155,9 +155,26 @@
     kv_heads = KVH // lax.axis_size("tp")
     bias_wide = qkv_bias.astype(jnp.float32)
     other_rows = from_partner(own_rows, "doc", 0)
-    both_full = lax.all_gather(
-        jnp.concatenate([own_rows, other_rows], axis=0), "tp", axis=1, tiled=True
+    value_2 = jnp.concatenate([own_rows, other_rows], axis=0)
+    count, index, width = (lax.axis_size("tp"), lax.axis_index("tp"), value_2.shape[1])
+    right = [(i, (i + 1) % count) for i in range(count)]
+    behind = [(i, (i - 1) % count) for i in range(count)]
+    both_full = jnp.zeros(
+        (*value_2.shape[:1], count * width, *value_2.shape[1 + 1 :]), value_2.dtype
     )
+    both_full = lax.dynamic_update_slice_in_dim(both_full, value_2, index * width, axis=1)
+    from_left = from_right = value_2
+    halfway = count // 2
+    for step in range(1, halfway + 1):
+        from_left = lax.ppermute(from_left, "tp", right)
+        both_full = lax.dynamic_update_slice_in_dim(
+            both_full, from_left, (index - step) % count * width, axis=1
+        )
+        if step < count - halfway:
+            from_right = lax.ppermute(from_right, "tp", behind)
+            both_full = lax.dynamic_update_slice_in_dim(
+                both_full, from_right, (index + step) % count * width, axis=1
+            )
     normed = rms_norm(both_full, norm_gain)
     full_weight = lax.all_gather(qkv_weight, "doc", axis=0, tiled=True)
     both_sum = jnp.dot(normed, full_weight, preferred_element_type=jnp.float32)

time: 323 us -> 255 us (0.79)
  waiting for transfers between devices: 177 us -> 99.2 us
  local copies, waits for them, and re-layouts: 30.7 us -> 40 us
  other arithmetic: 42.6 us -> 39 us
    all_gather x1, waiting for transfers between devices: 82.3 us -> 0.02 us  [shards(): full_weight = lax.all_gather(qkv_weight, 'doc', axis=0, tiled=True)]
    ppermute x0 -> x3, waiting for transfers between devices: none -> 66.5 us  [the longest x2 66.5 us: shards(): from_left = lax.ppermute(from_left, 'tp', right)]
    all_gather x1 -> x0, waiting for transfers between devices: 63.3 us -> none  [shards(): lax.all_gather(jnp.concatenate([own_rows, other_rows], axis=0), 'tp', axi...]
    dynamic_update_slice x0 -> x4, local copies, waits for them, and re-layouts: none -> 5.69 us  [the longest x2 3.59 us: shards(): lax.dynamic_update_slice_in_dim(both_full, from_left, (index - step) % co...]
  transfers between devices with their start and end apart: 5 -> 7, of which waited for: 5 -> 5; matrix products, arithmetic and copies ran while one was open for 5% -> 13% of each run, Pallas kernels for 0% -> 0%
where the time goes in v1:
time: 255 us; the launch traced here: 253 us
  waiting for transfers between devices  99.2 us (39%)
  local copies, waits for them, and re-layouts  40 us (16%)
  other arithmetic  39 us (15%)
  matrix products  35.4 us (14%)
  starting transfers between devices  22.7 us (9%)
  between operations  17.1 us (7%)
    ppermute x2, waiting for transfers between devices, shards(): from_left = lax.ppermute(from_left, 'tp', right)  66.5 us
    all_to_all x1, waiting for transfers between devices, shards(): lax.all_to_all(send_rows, 'doc', split_axis=0, concat_axis=0, tiled=True)  24.8 us
    dot_general x1, matrix products, shards(): both_sum = jnp.dot(normed, full_weight, preferred_element_type=jnp.float32)  15.6 us
    all_to_all x1, starting transfers between devices, shards(): lax.all_to_all(send_pos, 'doc', split_axis=0, concat_axis=0, tiled=True)  13.2 us
    dot_general x2, matrix products, attention(): jnp.einsum('kgqs,skd->qkgd', probabilities, value_heads[:row_stop], prefe...  12 us
    convert_element_type x2, local copies, waits for them, and re-layouts, rotate(): widened = heads.astype(jnp.float32)  10.1 us
    reduce_sum x2, other arithmetic, attention(): jnp.sum(exponent, axis=-1, keepdims=True)  9.7 us
    dot_general x2, matrix products, attention(): jnp.einsum('qkgd,skd->kgqs', grouped[row_start:row_stop], key_heads[:row_...  7.79 us
  transfers between devices with their start and end apart: 7, of which 5 were waited for; matrix products, arithmetic and copies ran while one was open for 13% of the time, Pallas kernels for 0%

profile of v1, /device:TPU:1, one launch (start us, length us, event | category | flops | bytes accessed | tf_op | source)
XLA Modules:
  0.0 253.3 jit_solution(271130184569147530)
XLA Ops:
  6.5 0.7 all-gather.2.cloned.1.call-update
  7.3 0.7 fusion.55
  8.1 0.1 reduce.4
  8.2 0.7 iota_minimum_fusion
  8.9 0.2 select_reduce_fusion.2
  9.1 0.7 add_subtract_fusion
  9.8 0.8 select_reduce_fusion
  10.5 0.7 fusion.61
  11.2 1.2 reduce-window.20
  12.5 0.2 slice_reduce_fusion
  12.7 0.7 broadcast_compare_fusion
  13.4 0.1 fusion.44
  13.5 0.7 compare_select_fusion.1
  14.2 2.6 %scatter_custom_fusion = s32[512]{0:T(512)S(1)} fusion(s32[512]{0:T(512)S(1)} %compare_select_fusion.1, s32[512]{0:T(512)} %param.10, s32[]{:T(128)} %constant.74.clone.1), kind=kCustom, calls=%fused_computation.98 | custom fusion | bytes 2560 | tf_op jit(solution)/shard_map/scatter | solution.py:144
  16.8 0.7 all_to_all.9
  17.5 13.2 %all-to-all-start = ((s32[64,1,8]{2,1,0:T(1,128)}), s32[64,1,8]{2,1,0:T(1,128)S(1)}, u32[]{:S(2)}, u32[]{:S(2)}) async-start(s32[64,1,8]{2,1,0:T(1,128)} %bitcast.4), calls=%async_computation | async-start | bytes 65536 | tf_op jit(solution)/shard_map/all_to_all | solution.py:149
  30.7 4.3 %scatter_custom_fusion.1 = bf16[512,896]{1,0:T(8,128)(2,1)} fusion(s32[512]{0:T(512)S(1)} %compare_select_fusion.1, bf16[512,896]{1,0:T(8,128)(2,1)} %param.8, bf16[]{:T(256)} %constant.73.clone.1), kind=kCustom, calls=%fused_computation.62 | custom fusion | bytes 918016 | tf_op jit(solution)/shard_map/scatter | solution.py:59
  34.9 5.1 %all-to-all-done = s32[64,1,8]{2,1,0:T(1,128)S(1)} async-done(((s32[64,1,8]{2,1,0:T(1,128)}), s32[64,1,8]{2,1,0:T(1,128)S(1)}, u32[]{:S(2)}, u32[]{:S(2)}) %all-to-all-start) | async-done | bytes 2080 | tf_op jit(solution)/shard_map/all_to_all | solution.py:149
  40.0 5.2 %all-to-all-start.1 = ((bf16[64,8,896]{2,1,0:T(8,128)(2,1)}), bf16[64,8,896]{2,1,0:T(8,128)(2,1)S(1)}, u32[]{:S(2)}, u32[]{:S(2)}) async-start(bf16[64,8,896]{2,1,0:T(8,128)(2,1)} %bitcast.6), calls=%async_computation.1 | async-start | bytes 1835008 | tf_op jit(solution)/shard_map/all_to_all | solution.py:148
  45.3 0.5 broadcast.176
  45.8 0.6 reduce.10
  46.5 24.8 %all-to-all-done.1 = bf16[64,8,896]{2,1,0:T(8,128)(2,1)S(1)} async-done(((bf16[64,8,896]{2,1,0:T(8,128)(2,1)}), bf16[64,8,896]{2,1,0:T(8,128)(2,1)S(1)}, u32[]{:S(2)}, u32[]{:S(2)}) %all-to-all-start.1) | async-done | bytes 917536 | tf_op jit(solution)/shard_map/all_to_all | solution.py:148
  71.3 2.9 %scatter_custom_fusion.2 = bf16[512,896]{1,0:T(8,128)(2,1)S(1)} fusion(s32[512]{0:T(512)S(1)} %bitcast.108, bf16[64,8,896]{2,1,0:T(8,128)(2,1)S(1)} %all-to-all-done.1, bf16[]{:T(256)} %constant.73.clone.1), kind=kCustom, calls=%fused_computation.46 | custom fusion | bytes 1835010 | tf_op jit(solution)/shard_map/scatter | solution.py:59
  74.3 1.6 collective-permute-start
  75.9 2.0 collective-permute-done
  78.0 0.1 constant_dynamic-update-slice_fusion
  78.1 1.2 collective-permute-start.1
  79.3 1.5 collective-permute-start.2
  80.8 0.1 select_reduce_fusion.1
  81.1 0.6 fusion.52
  81.7 39.0 %collective-permute-done.1 = bf16[1024,896]{1,0:T(8,128)(2,1)} collective-permute-done((bf16[1024,896]{1,0:T(8,128)(2,1)S(1)}, bf16[1024,896]{1,0:T(8,128)(2,1)}, u32[]{:S(2)}, u32[]{:S(2)}) %collective-permute-start.1) | collective-permute-done | bytes 1835040 | tf_op jit(solution)/shard_map/ppermute | solution.py:169
  120.7 1.3 fusion.51
  122.0 2.0 fusion.53
  127.4 0.1 fusion.27
  127.6 0.4 fusion.20
  128.0 2.7 %fusion.38 = (f32[1024,64]{1,0:T(8,128)S(1)}, f32[1024,64]{1,0:T(8,128)}) fusion(f32[64]{0:T(128)S(1)} %multiply_exponential_fusion), kind=kLoop, calls=%fused_computation.60 | loop fusion | flops 65536 | bytes 524544 | tf_op jit(solution)/shard_map/cos | solution.py:39
  130.6 0.5 broadcast_in_dim.61
  131.1 0.3 constant_dynamic-update-slice_fusion.5
  131.4 1.8 constant_dynamic-update-slice_fusion.4
  133.2 1.8 constant_dynamic-update-slice_fusion.3
  135.1 27.5 %collective-permute-done.3 = bf16[1024,896]{1,0:T(8,128)(2,1)} collective-permute-done((bf16[1024,896]{1,0:T(8,128)(2,1)}, bf16[1024,896]{1,0:T(8,128)(2,1)}, u32[]{:S(2)}, u32[]{:S(2)}) %collective-permute-start.3) | collective-permute-done | bytes 1835040 | tf_op jit(solution)/shard_map/ppermute | solution.py:169
  162.5 1.8 constant_dynamic-update-slice_fusion.2
  164.4 3.0 %copy-done.1 = bf16[1024,3584]{1,0:T(8,128)(2,1)} copy-done((bf16[1024,3584]{1,0:T(8,128)(2,1)}, bf16[1024,3584]{1,0:T(8,128)(2,1)S(1)}, u32[]{:S(2)}) %copy-start.1) | copy-done | bytes 7340056
  167.3 1.5 fusion
  168.9 15.6 %broadcast_select_fusion = (bf16[1024,1152]{1,0:T(8,128)(2,1)}, bf16[1024,1152]{1,0:T(8,128)(2,1)S(1)}) fusion(pred[1024]{0:T(1024)(128)(4,1)S(1)} %copy-done.7, f32[1152]{0:T(1024)S(1)} %convert_element_type.67, bf16[3584,1152]{1,0:T(8,128)(2,1)} %all-gather.2.cloned.1.call-done, bf16[1024,3584]{1,0:T(8,128)(2,1)} %copy-done.1, ...), kind=kOutput, calls=%fused_computation.31 | convolution fusion | flops 8473935872 | bytes 20340224 | tf_op jit(solution)/shard_map/dot_general | solution.py:180
  184.6 6.3 %dynamic_update_slice.19 = bf16[1024,1152]{1,0:T(8,128)(2,1)} dynamic-update-slice(bf16[1024,1152]{1,0:T(8,128)(2,1)} %get-tuple-element.18, bf16[512,1152]{1,0:T(8,128)(2,1)S(1)} %slice.64, s32[]{:T(128)S(6)} %select_n.97, s32[]{:T(128)} %constant.69.clone.1) | dynamic-update-slice | bytes 2359300 | tf_op jit(solution)/shard_map/dynamic_update_slice | solution.py:64
  190.9 1.0 convert_bitcast_fusion
  191.9 3.6 %slice_convert_fusion = f32[1024,896]{1,0:T(8,128)} fusion(bf16[1024,1152]{1,0:T(8,128)(2,1)} %dynamic_update_slice.19), kind=kLoop, calls=%fused_computation.34 | loop fusion | flops 917504 | bytes 5505024 | tf_op jit(solution)/shard_map/convert_element_type | solution.py:45
  195.5 0.2 fusion.36
  195.7 5.1 %copy.47 = f32[1024,896]{0,1:T(8,128)} copy(f32[1024,896]{1,0:T(8,128)} %slice_convert_fusion) | data formatting | bytes 7340032 | tf_op jit(solution)/shard_map/convert_element_type | solution.py:45
  200.7 5.0 %copy.48 = f32[1024,7,128]{2,0,1:T(8,128)} copy(f32[1024,7,128]{0,2,1:T(8,128)} %bitcast.104) | data formatting | bytes 7340032 | tf_op jit(solution)/shard_map/convert_element_type | solution.py:45
  205.8 4.4 %slice_negate_fusion = (f32[1024,7,64]{2,0,1:T(8,128)S(1)}, f32[1024,7,64]{2,0,1:T(8,128)S(1)}) fusion(f32[1024,7,128]{2,0,1:T(8,128)} %copy.48), kind=kLoop, calls=%fused_computation.24 | loop fusion | flops 458752 | bytes 7340032 | tf_op jit(solution)/shard_map/neg | solution.py:47
  210.2 1.6 fusion.35
  211.8 0.5 copy-done
  212.3 1.1 fusion.16
  213.4 1.3 fusion.12
  214.7 1.5 fusion.11
  216.2 4.0 %fusion.22 = bf16[1,128,7,512]{3,1,2,0:T(8,128)(2,1)} fusion(f32[7,512]{1,0:T(8,128)S(1)} %fusion.11, f32[7,512]{1,0:T(8,128)S(1)} %get-tuple-element.22, f32[512,512,7]{1,0,2:T(8,128)S(1)} %get-tuple-element.23, pred[512,512]{0,1:T(8,128)(4,1)S(1)} %fusion.27, pred[512]{0:T(512)(128)(4,1)S(1)} %get-tuple-element.24, ...), kind=kOutput, calls=%fused_computation.39 | convolution fusion | flops 479854592 | bytes 8679936 | tf_op jit(solution)/shard_map/kgqs,skd->qkgd/dot_general | solution.py:105
  220.3 1.5 copy.55
  221.8 6.5 %fusion.4 = (f32[7,512]{1,0:T(8,128)S(1)}, f32[1024,512,7]{1,0,2:T(8,128)}) fusion(pred[512,1024]{0,1:T(8,128)(4,1)S(1)} %fusion.20, bf16[1024,7,128]{2,0,1:T(8,128)(2,1)S(1)} %fusion.16, bf16[1024,128]{1,0:T(8,128)(2,1)S(1)} %get-tuple-element.9), kind=kOutput, calls=%fused_computation.12 | convolution fusion | flops 950530560 | bytes 16398336 | tf_op jit(solution)/shard_map/qkgd,skd->kgqs/dot_general | solution.py:90
  228.4 8.2 %fusion.3 = f32[7,512]{1,0:T(8,128)S(1)} fusion(f32[1024,512,7]{1,0,2:T(8,128)} %get-tuple-element.21, f32[7,512]{1,0:T(8,128)S(1)} %get-tuple-element.20, pred[512,1024]{0,1:T(8,128)(4,1)S(1)} %fusion.20), kind=kLoop, calls=%fused_computation.11 | loop fusion | flops 14676480 | bytes 15233024 | tf_op jit(solution)/shard_map/reduce_sum | solution.py:104
  236.5 7.9 %fusion.21 = bf16[1,128,7,512]{3,1,2,0:T(8,128)(2,1)S(1)} fusion(f32[7,512]{1,0:T(8,128)S(1)} %fusion.3, f32[7,512]{1,0:T(8,128)S(1)} %get-tuple-element.20, f32[1024,512,7]{1,0,2:T(8,128)} %get-tuple-element.21, pred[512,1024]{0,1:T(8,128)(4,1)S(1)} %fusion.20, pred[512]{0:T(512)(128)(4,1)S(1)} %get-tuple-element.25, ...), kind=kOutput, calls=%fused_computation.37 | convolution fusion | flops 958791680 | bytes 16413184 | tf_op jit(solution)/shard_map/kgqs,skd->qkgd/dot_general | solution.py:105
  244.5 0.6 copy.56
  245.1 1.4 pad_maximum_fusion
  (34 shorter events, 0.6 us)
Async XLA Ops:
  6.5 162.3 %all-gather.2.cloned.1.call-start = ((), (), s32[]{:S(2)}) async-start(), calls=%async_computation.2 | async-start | bytes 8386560 | tf_op jit(solution)/shard_map/all_gather | solution.py:179
  7.3 73.8 %copy-start.3 = (bf16[3584]{0:T(1024)(128)(2,1)S(1)}, bf16[3584]{0:T(1024)(128)(2,1)}, u32[]{:S(2)}) copy-start(bf16[3584]{0:T(1024)(128)(2,1)} %param.13) | copy-start | bytes 21508
  7.9 73.1 %copy-start.4 = (bf16[1152]{0:T(1024)(128)(2,1)S(1)}, bf16[1152]{0:T(1024)(128)(2,1)}, u32[]{:S(2)}) copy-start(bf16[1152]{0:T(1024)(128)(2,1)} %param.15) | copy-start | bytes 6916
  8.0 112.7 %copy-start.6 = (s32[64]{0:T(128)S(1)}, s32[64]{0:T(128)}, u32[]{:S(2)}) copy-start(s32[64]{0:T(128)} %param.12) | copy-start | bytes 772
  8.0 114.0 %copy-start.5 = (s32[64]{0:T(128)S(1)}, s32[64]{0:T(128)}, u32[]{:S(2)}) copy-start(s32[64]{0:T(128)} %param.11) | copy-start | bytes 772
  17.5 22.5 %all-to-all-start = ((s32[64,1,8]{2,1,0:T(1,128)}), s32[64,1,8]{2,1,0:T(1,128)S(1)}, u32[]{:S(2)}, u32[]{:S(2)}) async-start(s32[64,1,8]{2,1,0:T(1,128)} %bitcast.4), calls=%async_computation | async-start | bytes 65536 | tf_op jit(solution)/shard_map/all_to_all | solution.py:149
  40.0 31.3 %all-to-all-start.1 = ((bf16[64,8,896]{2,1,0:T(8,128)(2,1)}), bf16[64,8,896]{2,1,0:T(8,128)(2,1)S(1)}, u32[]{:S(2)}, u32[]{:S(2)}) async-start(bf16[64,8,896]{2,1,0:T(8,128)(2,1)} %bitcast.6), calls=%async_computation.1 | async-start | bytes 1835008 | tf_op jit(solution)/shard_map/all_to_all | solution.py:148
  74.3 3.7 %collective-permute-start = (bf16[512,896]{1,0:T(8,128)(2,1)S(1)}, bf16[512,896]{1,0:T(8,128)(2,1)S(1)}, u32[]{:S(2)}, u32[]{:S(2)}) collective-permute-start(bf16[512,896]{1,0:T(8,128)(2,1)S(1)} %scatter_custom_fusion.2), channel_id=1, source_target_pairs={{0,4},{4,0},{8,12},{12,8},{16,20},{20,16},{24,28},{28,24},{32,36},... | collective-permute-start | bytes 2752520 | tf_op jit(solution)/shard_map/ppermute | solution.py:18
  78.1 42.6 %collective-permute-start.1 = (bf16[1024,896]{1,0:T(8,128)(2,1)S(1)}, bf16[1024,896]{1,0:T(8,128)(2,1)}, u32[]{:S(2)}, u32[]{:S(2)}) collective-permute-start(bf16[1024,896]{1,0:T(8,128)(2,1)S(1)} %constant_dynamic-update-slice_fusion), channel_id=1, source_target_pairs={{0,1},{1,2},{2,3},{3,0},{4,5},{5,6},{6,7},{7,4},{8,9},{9,10},{10,1... | collective-permute-start | bytes 5505032 | tf_op jit(solution)/shard_map/ppermute | solution.py:169
  79.3 53.9 %collective-permute-start.2 = (bf16[1024,896]{1,0:T(8,128)(2,1)S(1)}, bf16[1024,896]{1,0:T(8,128)(2,1)}, u32[]{:S(2)}, u32[]{:S(2)}) collective-permute-start(bf16[1024,896]{1,0:T(8,128)(2,1)S(1)} %constant_dynamic-update-slice_fusion), channel_id=1, source_target_pairs={{0,3},{1,0},{2,1},{3,2},{4,7},{5,4},{6,5},{7,6},{8,11},{9,8},{10,9... | collective-permute-start | bytes 5505032 | tf_op jit(solution)/shard_map/ppermute | solution.py:174
  120.7 41.8 %collective-permute-start.3 = (bf16[1024,896]{1,0:T(8,128)(2,1)}, bf16[1024,896]{1,0:T(8,128)(2,1)}, u32[]{:S(2)}, u32[]{:S(2)}) collective-permute-start(bf16[1024,896]{1,0:T(8,128)(2,1)} %collective-permute-done.1), channel_id=1, source_target_pairs={{0,1},{1,2},{2,3},{3,0},{4,5},{5,6},{6,7},{7,4},{8,9},{9,10},{10,1... | collective-permute-start | bytes 5505032 | tf_op jit(solution)/shard_map/ppermute | solution.py:169
  135.0 33.8 %copy-start.7 = (pred[1024]{0:T(1024)(128)(4,1)S(1)}, pred[1024]{0:T(1024)(128)(4,1)}, u32[]{:S(2)}) copy-start(pred[1024]{0:T(1024)(128)(4,1)} %constant.72.clone.1) | copy-start | bytes 3076
  164.3 3.0 %copy-start.1 = (bf16[1024,3584]{1,0:T(8,128)(2,1)}, bf16[1024,3584]{1,0:T(8,128)(2,1)S(1)}, u32[]{:S(2)}) copy-start(bf16[1024,3584]{1,0:T(8,128)(2,1)S(1)} %constant_dynamic-update-slice_fusion.2) | copy-start | bytes 22020100
  205.8 4.4 %copy-start.2 = (f32[1024,64]{1,0:T(8,128)S(1)}, f32[1024,64]{1,0:T(8,128)}, u32[]{:S(2)}) copy-start(f32[1024,64]{1,0:T(8,128)} %get-tuple-element.15) | copy-start | bytes 786436
  210.2 2.1 copy-start
Sparse Core Ops, SparseCore 0:
  10.0 89.1 all-gather.1
